TPU v7x, 768 devices: a whole 4x8x12 slice. The times are simulated.
768 devices in a mesh: ctx: 96 (over z, y), fsdp: 8 (over x, core).
Axes of the slice: x: 4, y: 8, z: 12, core: 2. Of those that a mesh axis runs over, the one named last changes fastest.
Arguments:
- values: bfloat16 [8, 12288, 4096], P('fsdp', 'ctx'), may hold values from -6 to 6
- cotangent: bfloat16 [8, 12288, 4096], P('fsdp', 'ctx'), may hold values from -6 to 6
- seg_ids: int32 [8, 12288], P('fsdp', 'ctx'), may hold values from 0 to 3, never falling along the last dimension, each value on 1 to 6144 neighbouring positions
- filters: bfloat16 [256, 128], P('fsdp'), may hold values from -0.5 to 0.5
- skip_gain: bfloat16 [4096], P('fsdp'), may hold values from -4 to 4
Outputs:
- mixed: bfloat16 [8, 12288, 4096], P('fsdp', 'ctx')
- grad_values: bfloat16 [8, 12288, 4096], P('fsdp', 'ctx')
- grad_filters: float32 [256, 128], P('fsdp')
- grad_skip: float32 [4096], P('fsdp')
Inputs may be any that keep to these rules, and one draw needn't show every extreme that they name: `seg_ids`: along each stream document numbers start at 0 and never fall; each document covers 1 to 6144 positions, and one covers exactly that many.
All inputs are finite; a program needn't handle non-finite values.
Results may differ from a plain program's by a relative error of at most 0.001.
Values may be sent and summed in bfloat16 or wider, within the bound.
A program may use at most 64 MiB of HBM per device.

v0:
```python
import jax
import jax.numpy as jnp
from jax import lax
from jax.sharding import PartitionSpec as P


def shifted(value, axis, by):
    peers = lax.axis_size(axis)
    pairs = [(i, i + by) for i in range(peers) if 0 <= i + by < peers]
    return lax.ppermute(value, axis, pairs)


def toeplitz(pattern, rows, width):
    count = pattern.shape[0]
    tiled = jnp.broadcast_to(pattern[:, None, :], (count, rows, width + 1)).reshape(
        count, rows * (width + 1)
    )
    return tiled[:, : rows * width].reshape(count, rows, width)


def diagonals(matrix, taps):
    count, rows, width = matrix.shape
    flat = jnp.concatenate(
        [matrix.reshape(count, rows * width), jnp.zeros((count, rows), matrix.dtype)], axis=1
    )
    bands = flat.reshape(count, rows, width + 1)[:, :, 1 : taps + 1]
    return jnp.sum(bands, axis=1)[:, ::-1]


def shards(values, cotangent, seg_ids, filters, skip_gain):
    local_vals = values[0]
    local_cot = cotangent[0]
    local_ids = seg_ids[0]
    rows, channels = local_vals.shape
    taps = filters.shape[1]
    filt, skip = (
        lax.all_gather(filters, "fsdp", axis=0, tiled=True),
        lax.all_gather(skip_gain, "fsdp", axis=0, tiled=True),
    )
    groups = filt.shape[0]
    gsize = channels // groups
    width = rows + taps
    tail_vals, tail_ids = shifted((local_vals, local_ids), "ctx", 1)
    vals_ext = jnp.concatenate([tail_vals, local_vals], axis=0)
    ids_prev = jnp.concatenate([tail_ids, local_ids], axis=0)
    same_prev = local_ids[:, None] == ids_prev[None, :]
    mask_half = same_prev.astype(jnp.bfloat16)
    mask_full = same_prev.astype(jnp.float32)
    block = min(64, groups)
    span = block * gsize
    skip_full = skip.astype(jnp.float32)
    row_block = max(min(32, rows), rows // 4)

    def one_block(index, carry):
        mixed_buf, adj_buf, fgrad, sgrad = carry
        first = index * block
        column = first * gsize
        fblk = lax.dynamic_slice_in_dim(filt, first, block, 0)
        lead = jnp.concatenate(
            [
                jnp.zeros((block, 1), jnp.bfloat16),
                fblk[:, ::-1],
                jnp.zeros((block, width - taps), jnp.bfloat16),
            ],
            axis=1,
        )
        forward = toeplitz(lead, rows, width) * mask_half[None]
        vblk = lax.dynamic_slice_in_dim(vals_ext, column, span, 1).reshape(width, block, gsize)
        own_vals = lax.dynamic_slice_in_dim(local_vals, column, span, 1)
        own_cot = lax.dynamic_slice_in_dim(local_cot, column, span, 1)
        cblk = own_cot.reshape(rows, block, gsize)
        skip_blk = lax.dynamic_slice_in_dim(skip_full, column, span, 0)
        conv = jnp.einsum(
            "gts,sgc->tgc", forward, vblk, preferred_element_type=jnp.float32
        ).reshape(rows, span)
        mixed_blk = (conv + skip_blk[None, :] * own_vals.astype(jnp.float32)).astype(jnp.bfloat16)
        skip_term = skip_blk[None, :] * own_cot.astype(jnp.float32)
        adj_blk = jnp.einsum(
            "gts,tgc->sgc", forward, cblk, preferred_element_type=jnp.float32
        ).reshape(width, span)
        adj_blk = adj_blk.at[taps:].add(skip_term)
        fsum = jnp.zeros((block, taps), jnp.float32)
        for offset in range(0, rows, row_block):
            cot_part = cblk[offset : offset + row_block]
            val_part = vblk[offset : offset + row_block + taps]
            mask_part = mask_full[offset : offset + row_block, offset : offset + row_block + taps]
            prod = (
                jnp.einsum("tgc,sgc->gts", cot_part, val_part, preferred_element_type=jnp.float32)
                * mask_part[None]
            )
            fsum = fsum + diagonals(prod, taps)
        mixed_buf = lax.dynamic_update_slice_in_dim(mixed_buf, mixed_blk, column, 1)
        adj_buf = lax.dynamic_update_slice_in_dim(adj_buf, adj_blk, column, 1)
        fgrad = lax.dynamic_update_slice_in_dim(fgrad, fsum, first, 0)
        sgrad = lax.dynamic_update_slice_in_dim(
            sgrad,
            jnp.sum(own_cot.astype(jnp.float32) * own_vals.astype(jnp.float32), axis=0),
            column,
            0,
        )
        return (mixed_buf, adj_buf, fgrad, sgrad)

    init = (
        jnp.zeros((rows, channels), jnp.bfloat16),
        jnp.zeros((width, channels), jnp.float32),
        jnp.zeros((groups, taps), jnp.float32),
        jnp.zeros((channels,), jnp.float32),
    )
    mixed_buf, adj_buf, fgrad, sgrad = lax.fori_loop(0, groups // block, one_block, init)
    spill = shifted(adj_buf[:taps], "ctx", -1)
    adjoint = adj_buf[taps:].at[rows - taps :].add(spill)
    grad_vals = adjoint.astype(jnp.bfloat16)
    shard_f, shard_s = (
        lax.psum_scatter(fgrad, "fsdp", scatter_dimension=0, tiled=True),
        lax.psum_scatter(sgrad, "fsdp", scatter_dimension=0, tiled=True),
    )
    total_f, total_s = lax.psum((shard_f, shard_s), "ctx")
    stream_count = lax.axis_size("fsdp")
    seq_length = rows * lax.axis_size("ctx")
    total_f = total_f / jnp.sqrt(jnp.float32(stream_count * seq_length * gsize))
    total_s = total_s / jnp.sqrt(jnp.float32(stream_count * seq_length))
    return (mixed_buf[None], grad_vals[None], total_f, total_s)


def solution(mesh):
    placed = (
        P("fsdp", "ctx", None),
        P("fsdp", "ctx", None),
        P("fsdp", "ctx"),
        P("fsdp", None),
        P("fsdp"),
    )
    return jax.shard_map(
        shards,
        mesh=mesh,
        in_specs=placed,
        out_specs=(P("fsdp", "ctx", None), P("fsdp", "ctx", None), P("fsdp", None), P("fsdp")),
        check_vma=False,
    )
```

profile of v0, /device:TPU:2, one launch (start us, length us, event | category | flops | bytes accessed | tf_op | source)
XLA Modules:
  0.0 772.3 jit_solution(9427307171723863192)
XLA Ops:
  7.2 2.3 copy.19
  9.6 3.5 collective-permute-start
  13.1 3.4 collective-permute-start.1
  16.6 15.8 %all_gather.6 = bf16[256,128]{1,0:T(8,128)(2,1)} all-gather(bf16[32,128]{1,0:T(8,128)(2,1)S(1)} %copy-done.5), channel_id=1, replica_groups=mesh['ctx'=96,'fsdp'=8] {'fsdp'}, dimensions={0}, use_global_device_ids=true | all-gather | bytes 73728 | tf_op jit(solution)/shard_map/all_gather | solution.py:37
  32.4 12.2 %all-gather = bf16[8,1,512]{2,1,0:T(2,128)(2,1)S(1)} all-gather(bf16[1,1,512]{2,1,0:T(2,128)(2,1)S(1)} %reshape.284), channel_id=1, replica_groups=mesh['ctx'=96,'fsdp'=8] {'fsdp'}, dimensions={0}, use_global_device_ids=true | all-gather | bytes 9216 | tf_op jit(solution)/shard_map/all_gather | solution.py:38
  50.1 2.6 broadcast_in_dim.58.clone
  55.0 241.8 %while.25 = (s32[]{:T(128)}, bf16[128,4096]{1,0:T(8,128)(2,1)}, f32[256,4096]{1,0:T(8,128)}, f32[256,128]{1,0:T(8,128)}, f32[4096]{0:T(1024)}, /*index=5*/bf16[2...) while((s32[]{:T(128)}, bf16[128,4096]{1,0:T(8,128)(2,1)}, ...), condition=%wide.region_6.7_spmd.clone, body=%wide.region_0.6_spmd.clone.sunk | while | flops 182082944 | bytes 126698264 | solution.py:109
  55.0 2.0 fusion.61
  57.0 2.6 fusion.60
  62.8 2.9 reshape.315
  70.0 2.9 reshape.317
  76.7 2.9 reshape.319
  83.4 2.9 reshape.321
  89.4 3.2 broadcast_in_dim.65
  92.6 10.8 %reshape.313 = bf16[64,32896]{1,0:T(8,128)(2,1)} reshape(bf16[64,128,257]{2,1,0:T(8,128)(2,1)} %broadcast_in_dim.65) | data formatting | bytes 8421376 | tf_op jit(solution)/shard_map/while/body/eval_jaxpr/reshape | solution.py:15
  103.4 2.2 slice-done
  115.5 2.0 fusion.61
  117.5 2.7 fusion.60
  123.4 2.9 reshape.315
  130.6 2.9 reshape.317
  137.3 2.9 reshape.319
  143.9 2.9 reshape.321
  150.0 3.2 broadcast_in_dim.65
  153.2 10.8 %reshape.313 = bf16[64,32896]{1,0:T(8,128)(2,1)} reshape(bf16[64,128,257]{2,1,0:T(8,128)(2,1)} %broadcast_in_dim.65) | data formatting | bytes 8421376 | tf_op jit(solution)/shard_map/while/body/eval_jaxpr/reshape | solution.py:15
  164.0 2.2 slice-done
  176.0 2.0 fusion.61
  178.0 2.6 fusion.60
  183.8 2.9 reshape.315
  191.1 2.9 reshape.317
  197.7 2.9 reshape.319
  204.4 2.9 reshape.321
  210.4 3.2 broadcast_in_dim.65
  213.6 10.8 %reshape.313 = bf16[64,32896]{1,0:T(8,128)(2,1)} reshape(bf16[64,128,257]{2,1,0:T(8,128)(2,1)} %broadcast_in_dim.65) | data formatting | bytes 8421376 | tf_op jit(solution)/shard_map/while/body/eval_jaxpr/reshape | solution.py:15
  224.4 2.2 slice-done
  236.4 2.0 fusion.61
  238.5 2.6 fusion.60
  244.2 2.9 reshape.315
  251.5 2.9 reshape.317
  258.1 2.9 reshape.319
  264.8 2.9 reshape.321
  270.8 3.2 broadcast_in_dim.65
  274.0 10.8 %reshape.313 = bf16[64,32896]{1,0:T(8,128)(2,1)} reshape(bf16[64,128,257]{2,1,0:T(8,128)(2,1)} %broadcast_in_dim.65) | data formatting | bytes 8421376 | tf_op jit(solution)/shard_map/while/body/eval_jaxpr/reshape | solution.py:15
  284.8 2.2 slice-done
  296.8 3.2 slice.251
  303.2 22.6 %all-reduce.4 = f32[4096]{0:T(1024)S(1)} all-reduce(f32[4096]{0:T(1024)S(1)} %copy-done.4), channel_id=3, replica_groups=mesh['ctx'=96,'fsdp'=8] {'fsdp'}, use_global_device_ids=true, to_apply=%region_9.0.clone | all-reduce | flops 4096 | bytes 32768
  325.9 16.4 %reduce-scatter.2.cloned.1.call-done = f32[32,128]{1,0:T(8,128)} async-done(((f32[256,128]{1,0:T(8,128)}), f32[32,128]{1,0:T(8,128)}) %reduce-scatter.2.cloned.1.call-update) | async-done | bytes 16400 | tf_op jit(solution)/shard_map/reduce_scatter | solution.py:114
  342.3 419.2 %all-reduce.5 = (f32[32,128]{1,0:T(8,128)S(1)}, f32[512]{0:T(512)S(1)}) all-reduce(f32[32,128]{1,0:T(8,128)} %reduce-scatter.2.cloned.1.call-done, f32[512]{0:T(512)S(1)} %dynamic-slice.23), channel_id=1, replica_groups=mesh['ctx'=96,'fsdp'=8] {'ctx'}, use_global_device_ids=true, to_apply=%region_8.0 | all-reduce | flops 4608 | bytes 36864 | tf_op jit(solution)/shard_map/psum | solution.py:117
  762.7 2.8 fusion.7
  (227 shorter events, 123.3 us)
Async XLA Ops:
  7.2 9.4 %copy-start.6 = (bf16[512]{0:T(512)(128)(2,1)S(1)}, bf16[512]{0:T(512)(128)(2,1)}, u32[]{:S(2)}) copy-start(bf16[512]{0:T(512)(128)(2,1)} %param.17) | copy-start | bytes 3076
  7.2 9.4 %copy-start.5 = (bf16[32,128]{1,0:T(8,128)(2,1)S(1)}, bf16[32,128]{1,0:T(8,128)(2,1)}, u32[]{:S(2)}) copy-start(bf16[32,128]{1,0:T(8,128)(2,1)} %param.16) | copy-start | bytes 24580
  7.2 37.4 %copy-start.3 = (bf16[1,128,4096]{2,1,0:T(8,128)(2,1)S(1)}, bf16[1,128,4096]{2,1,0:T(8,128)(2,1)}, u32[]{:S(2)}) copy-start(bf16[1,128,4096]{2,1,0:T(8,128)(2,1)} %param.14) | copy-start | bytes 3145732
  7.2 335.1 %reduce-scatter.2.cloned.1.call-start = ((), (), s32[]{:S(2)}) async-start(), calls=%async_computation.1 | async-start | bytes 147456 | tf_op jit(solution)/shard_map/reduce_scatter | solution.py:114
  9.6 39.0 %collective-permute-start = (bf16[128,4096]{0,1:T(8,128)(2,1)}, bf16[128,4096]{0,1:T(8,128)(2,1)S(1)}, u32[]{:S(2)}, u32[]{:S(2)}) collective-permute-start(bf16[128,4096]{0,1:T(8,128)(2,1)} %bitcast), channel_id=1, source_target_pairs={{0,8},{8,16},{16,24},{24,32},{32,40},{40,48},{48,56},{56,64},{64,7... | collective-permute-start | bytes 3145736 | tf_op jit(solution)/shard_map/ppermute | solution.py:10
  13.1 32.8 %collective-permute-start.1 = (s32[128]{0:T(128)}, s32[128]{0:T(128)S(1)}, u32[]{:S(2)}, u32[]{:S(2)}) collective-permute-start(s32[128]{0:T(128)} %bitcast.3), channel_id=1, source_target_pairs={{0,8},{8,16},{16,24},{24,32},{32,40},{40,48},{48,56},{56,64},{64,7... | collective-permute-start | bytes 1544 | tf_op jit(solution)/shard_map/ppermute | solution.py:10
  55.0 2.0 copy-start
  83.4 3.3 copy-start.2
  103.4 2.2 slice-start
  112.0 3.5 copy-start.1
  115.5 2.0 copy-start
  143.9 3.3 copy-start.2
  164.0 2.2 slice-start
  172.6 3.4 copy-start.1
  176.0 2.0 copy-start
  204.4 3.3 copy-start.2
  224.4 2.2 slice-start
  233.0 3.4 copy-start.1
  236.4 2.0 copy-start
  264.8 3.3 copy-start.2
  284.8 2.2 slice-start
  293.4 3.4 copy-start.1
  296.8 6.4 copy-start.4
  300.0 462.7 %collective-permute-start.2 = (f32[128,4096]{1,0:T(8,128)}, f32[128,4096]{1,0:T(8,128)S(1)}, u32[]{:S(2)}, u32[]{:S(2)}) collective-permute-start(f32[128,4096]{1,0:T(8,128)} %slice.251), channel_id=1, source_target_pairs={{8,0},{16,8},{24,16},{32,24},{40,32},{48,40},{56,48},{64,56},{72,6... | collective-permute-start | bytes 6291464 | tf_op jit(solution)/shard_map/ppermute | solution.py:10
Sparse Core Ops, SparseCore 0:
  301.4 40.8 reduce-scatter.1
where the time goes:
time: 775 us; the launch traced here: 772 us
  blocking collectives  470 us (61%)
  local copies, waits for them, and re-layouts  205 us (26%)
  matrix products  28.9 us (4%)
  other arithmetic  28.6 us (4%)
  waiting for transfers between devices  16.4 us (2%)
  between operations  14.8 us (2%)
  starting transfers between devices  8.27 us (1%)
    psum x1, blocking collectives, shards(): total_f, total_s = lax.psum((shard_f, shard_s), 'ctx')  419 us
    reshape x16, local copies, waits for them, and re-layouts, diagonals(): bands = flat.reshape(count, rows, width + 1)[:, :, 1:taps + 1]  45.7 us
    reshape x4, local copies, waits for them, and re-layouts, toeplitz(): jnp.broadcast_to(pattern[:, None, :], (count, rows, width + 1))  43.3 us
    reshape x16, local copies, waits for them, and re-layouts, diagonals(): matrix.reshape(count, rows * width)  26.1 us
    unnamed x1, blocking collectives  22.6 us
    dot_general x16, matrix products, one_block(): jnp.einsum('tgc,sgc->gts', cot_part, val_part, preferred_element_type=jnp...  21.4 us
    reduce_scatter x1, waiting for transfers between devices, shards(): lax.psum_scatter(fgrad, 'fsdp', scatter_dimension=0, tiled=True)  16.4 us
    all_gather x1, blocking collectives, shards(): lax.all_gather(filters, 'fsdp', axis=0, tiled=True)  15.8 us
  transfers between devices with their start and end apart: 4, of which 1 were waited for; matrix products, arithmetic and copies ran while one was open for 1% of the time, Pallas kernels for 0%

commit v1 on v0

v1 whole, which is shorter than its diff:
```python
import jax
import jax.numpy as jnp
from jax import lax
from jax.experimental import pallas as pl
from jax.experimental.pallas import tpu as pltpu
from jax.sharding import PartitionSpec as P

MESH = pl.DeviceIdType.MESH
F32 = jnp.float32
BF16 = jnp.bfloat16
LANES = 128
CHUNKS = 8
PARTS = 8
ROWS_Y = 8
ROWS_Z = 12
PACK = 40
PER = 4
HALF = CHUNKS // 2
ORDER_V = (0, 1, 2, 3, 4, 5, 6, 7)
ORDER_C = (4, 5, 6, 7, 0, 1, 2, 3)
ORDER_A = (0, 4, 1, 5, 2, 6, 3, 7)
SEGMENTS = ((0, 2), (2, 5), (5, 8))


def columns(block):
    return pl.ds(pl.multiple_of(block * LANES, LANES), LANES)


def set_masks(ids, bmask, fmask):
    row = lax.broadcasted_iota(jnp.int32, (LANES, LANES), 0)
    col = lax.broadcasted_iota(jnp.int32, (LANES, LANES), 1)
    prev, own, later = [jnp.broadcast_to(x.astype(F32), (LANES, LANES)) for x in ids]
    mine = own.T
    kept = (
        (col <= row) & (own == mine),
        (col > row) & (prev == mine),
        (col >= row) & (own == mine),
        (col < row) & (later == mine),
    )
    for k in range(4):
        mask = jnp.where(kept[k], 1.0, 0.0)
        fmask[k] = mask
        bmask[k] = mask.astype(BF16)


def filter_block(chunk, inner, left, own, halo, first, fmask, pack, sums):
    cols = columns(chunk * PER + inner)
    group = lax.shift_right_logical(lax.broadcasted_iota(jnp.int32, (LANES, LANES), 1), 4)
    x = left[:, cols]
    y = own[:, cols]
    lhs = jnp.concatenate([jnp.where(group == g, x, jnp.zeros_like(x)) for g in range(8)], axis=0)
    rhs = jnp.concatenate([y, halo[:, cols]], axis=0)
    prod = lax.dot_general(lhs, rhs, (((1,), (1,)), ((), ())), preferred_element_type=F32)
    for g in range(8):
        part = prod[g * LANES : (g + 1) * LANES]
        kept = part[:, :LANES] * fmask[first] + part[:, LANES:] * fmask[first + 1]
        total = kept[0:8]
        for a in range(1, 16):
            total = total + pltpu.roll(kept[8 * a : 8 * a + 8], LANES - 8 * a, 1)
        sums[8 * g : 8 * g + 8] = total
    total = sums[pl.ds(0, 8, stride=8)]
    for b in range(1, 8):
        total = total + pltpu.roll(sums[pl.ds(b, 8, stride=8)], LANES - b, 1)
    pack[chunk, pl.ds(pl.multiple_of(inner * 8, 8), 8)] = total
    pack[chunk, pl.ds(32 + inner, 1)] = jnp.sum(x.astype(F32) * y.astype(F32), axis=0, keepdims=True)


def build(block, filt, flip, bmask, lhs):
    rows = pl.ds(pl.multiple_of(block * 8, 8), 8)
    taps = filt[rows]
    mirror = flip[rows]
    for g in range(8):
        spot = pl.ds(g * LANES, LANES)
        for source, first in ((mirror, 0), (taps, 2)):
            base = pltpu.roll(jnp.broadcast_to(source[g : g + 1], (8, LANES)), 0, 1, stride=1, stride_axis=0)
            circ = jnp.concatenate([base] + [pltpu.roll(base, 8 * a, 1) for a in range(1, 16)], axis=0).astype(BF16)
            lhs[first, spot] = circ * bmask[first]
            lhs[first + 1, spot] = circ * bmask[first + 1]


def apply(block, lhs, skips, vals, vprev, cot, cnext, mix, grad):
    cols = columns(block)
    group = lax.shift_right_logical(lax.broadcasted_iota(jnp.int32, (LANES, LANES), 1), 4)
    skip = skips[block // PER, pl.ds(lax.rem(block, PER), 1)]
    for first, own, halo, out in ((0, vals, vprev, mix), (2, cot, cnext, grad)):
        mine = own[:, cols]
        rhs = jnp.concatenate([mine, halo[:, cols]], axis=0)
        full = jnp.dot(jnp.concatenate([lhs[first], lhs[first + 1]], axis=1), rhs, preferred_element_type=F32)
        kept = full[0:LANES]
        for g in range(1, 8):
            kept = jnp.where(group == g, full[g * LANES : (g + 1) * LANES], kept)
        out[:, cols] = (kept + skip * mine.astype(F32)).astype(BF16)


def kernel(
    vals_hbm, cot_hbm, filt_ref, skip_ref, ids_ref, mix_hbm, grad_hbm, f_out, s_out,
    vals, cot, vprev, cnext, mix, grad, filt_all, skip_all, ids_buf, filt, flip, skips, bmask, fmask,
    lhs_a, lhs_b, sums_a, sums_b, pack, buf_x, buf_y, buf_z, part,
    load, send_v, recv_v, send_c, recv_c, send_f, recv_f, send_s, recv_s, send_i, recv_i,
    send_x, recv_x, send_y, recv_y, send_z, recv_z,
):
    ctx = lax.axis_index("ctx")
    me = lax.axis_index("fsdp")
    n = lax.axis_size("ctx")
    z, y = ctx // ROWS_Y, lax.rem(ctx, ROWS_Y)
    on_x = [(ctx, lax.rem(me + k, PARTS)) for k in range(1, PARTS)]
    on_z = [(lax.rem(z + k, ROWS_Z) * ROWS_Y + y, me) for k in range(1, ROWS_Z)]
    on_y = [(z * ROWS_Y + lax.rem(y + k, ROWS_Y), me) for k in range(1, ROWS_Y)]
    after = (lax.rem(ctx + 1, n), me)
    before = (lax.rem(ctx + n - 1, n), me)

    loads = [
        pltpu.make_async_copy(vals_hbm, vals, load.at[0]),
        pltpu.make_async_copy(cot_hbm, cot, load.at[1]),
    ]
    for copy in loads:
        copy.start()

    barrier = pltpu.get_barrier_semaphore()
    greeted = [after, before] + on_x + on_y + on_z
    for peer in greeted:
        pl.semaphore_signal(barrier, inc=1, device_id=peer, device_id_type=MESH)
    pl.semaphore_wait(barrier, len(greeted))

    def remote(src, dst, send, recv, peer):
        return pltpu.make_async_remote_copy(
            src_ref=src, dst_ref=dst, send_sem=send, recv_sem=recv, device_id=peer, device_id_type=MESH
        )

    small = [
        remote(ids_ref, ids_buf.at[0], send_i.at[0], recv_i.at[0], after),
        remote(ids_ref, ids_buf.at[1], send_i.at[1], recv_i.at[1], before),
    ]
    for copy in small:
        copy.start()
    width = PER * LANES
    v_copies, c_copies = {}, {}
    for k in range(CHUNKS):
        cut = pl.ds(ORDER_V[k] * width, width)
        v_copies[ORDER_V[k]] = remote(vals_hbm.at[:, cut], vprev.at[:, cut], send_v.at[k], recv_v.at[k], after)
        v_copies[ORDER_V[k]].start()
        cut = pl.ds(ORDER_C[k] * width, width)
        c_copies[ORDER_C[k]] = remote(cot_hbm.at[:, cut], cnext.at[:, cut], send_c.at[k], recv_c.at[k], before)
        c_copies[ORDER_C[k]].start()

    def spread(source_of, peers, mine, buf, send, recv, own):
        copies = []
        for k, peer in enumerate(peers):
            copies.append(remote(source_of(peer), buf.at[mine], send.at[k], recv.at[mine], peer))
            copies[-1].start()
        buf[mine] = own
        return copies

    def gathered(copies, peers, mine, buf, send, recv):
        count = len(peers) + 1
        for k in range(1, count):
            slot = lax.rem(mine + k, count)
            remote(buf.at[slot], buf.at[slot], send.at[k - 1], recv.at[slot], peers[k - 1]).wait_recv()
        for copy in copies:
            copy.wait_send()

    def summed(buf, count):
        total = buf[0]
        for k in range(1, count):
            total = total + buf[k]
        return total

    f_copies = spread(lambda peer: filt_ref, on_x, me, filt_all, send_f, recv_f, filt_ref[...])
    s_copies = spread(lambda peer: skip_ref, on_x, me, skip_all, send_s, recv_s, skip_ref[...])
    for k in range(PARTS):
        pack[k, 32:PACK] = jnp.zeros((PACK - 32, LANES), F32)

    for copy in small:
        copy.wait()
    none = jnp.full((1, LANES), -1, jnp.int32)
    set_masks(
        (jnp.where(ctx == 0, none, ids_buf[0]), ids_ref[...], jnp.where(ctx == n - 1, none, ids_buf[1])),
        bmask, fmask,
    )
    for copy in loads:
        copy.wait()

    for chunk in ORDER_A:
        if chunk < HALF:
            v_copies[chunk].wait_recv()
            refs = (cot, vals, vprev, 0)
        else:
            c_copies[chunk].wait_recv()
            refs = (vals, cot, cnext, 2)

        def two(j, carry, chunk=chunk, refs=refs):
            filter_block(chunk, 2 * j, *refs, fmask, pack, sums_a)
            filter_block(chunk, 2 * j + 1, *refs, fmask, pack, sums_b)
            return carry

        lax.fori_loop(0, PER // 2, two, 0)

    x_copies = spread(lambda peer: pack.at[peer[1]], on_x, me, buf_x, send_x, recv_x, pack[me])

    gathered(f_copies, on_x, me, filt_all, send_f, recv_f)
    gathered(s_copies, on_x, me, skip_all, send_s, recv_s)
    row = lax.broadcasted_iota(jnp.int32, (LANES, LANES), 0)
    col = lax.broadcasted_iota(jnp.int32, (LANES, LANES), 1)
    turn = jnp.where(((row + col) & (LANES - 1)) == 0, 1.0, 0.0).astype(BF16)
    for k in range(PARTS):
        skips[k] = skip_all[k].astype(F32)
        filt[32 * k : 32 * k + 32] = filt_all[k].astype(F32)
        flip[32 * k : 32 * k + 32] = jnp.dot(filt_all[k], turn, preferred_element_type=F32)
    for chunk in range(CHUNKS):
        if chunk < HALF:
            c_copies[chunk].wait_recv()
        else:
            v_copies[chunk].wait_recv()

    build(0, filt, flip, bmask, lhs_a)
    last = CHUNKS * PER - 1
    stores = []

    def segment(first, stop):
        def two(j, carry):
            block = first * PER + 2 * j
            build(block + 1, filt, flip, bmask, lhs_b)
            apply(block, lhs_a, skips, vals, vprev, cot, cnext, mix, grad)
            build(jnp.minimum(block + 2, last), filt, flip, bmask, lhs_a)
            apply(block + 1, lhs_b, skips, vals, vprev, cot, cnext, mix, grad)
            return carry

        lax.fori_loop(0, (stop - first) * PER // 2, two, 0)
        cut = pl.ds(first * width, (stop - first) * width)
        k = 2 + len(stores)
        for source, target in ((mix, mix_hbm), (grad, grad_hbm)):
            stores.append(pltpu.make_async_copy(source.at[:, cut], target.at[:, cut], load.at[k]))
            stores[-1].start()
            k += 1

    segment(*SEGMENTS[0])
    gathered(x_copies, on_x, me, buf_x, send_x, recv_x)
    part[0] = summed(buf_x, PARTS)
    y_copies = spread(lambda peer: part.at[0], on_y, y, buf_y, send_y, recv_y, part[0])
    segment(*SEGMENTS[1])
    gathered(y_copies, on_y, y, buf_y, send_y, recv_y)
    part[1] = summed(buf_y, ROWS_Y)
    z_copies = spread(lambda peer: part.at[1], on_z, z, buf_z, send_z, recv_z, part[1])
    segment(*SEGMENTS[2])
    gathered(z_copies, on_z, z, buf_z, send_z, recv_z)
    total = summed(buf_z, ROWS_Z)
    f_out[...] = total[0:32]
    s_out[...] = total[32:36]
    for chunk in range(CHUNKS):
        v_copies[chunk].wait_send()
        c_copies[chunk].wait_send()
    for copy in stores:
        copy.wait()


def shards(values, cotangent, seg_ids, filters, skip_gain):
    vals, cot = values[0], cotangent[0]
    rows, channels = vals.shape
    vm = pl.BlockSpec(memory_space=pltpu.VMEM)
    hbm = pl.BlockSpec(memory_space=pl.ANY)
    wide = pltpu.VMEM((rows, channels), BF16)
    dma = pltpu.SemaphoreType.DMA
    groups = channels // 16
    mixed, grad, total_f, total_s = pl.pallas_call(
        kernel,
        out_shape=(
            jax.ShapeDtypeStruct((rows, channels), BF16),
            jax.ShapeDtypeStruct((rows, channels), BF16),
            jax.ShapeDtypeStruct((32, LANES), F32),
            jax.ShapeDtypeStruct((PER, LANES), F32),
        ),
        in_specs=[hbm, hbm, vm, vm, vm],
        out_specs=(hbm, hbm, vm, vm),
        scratch_shapes=[
            wide, wide, wide, wide, wide, wide,
            pltpu.VMEM((PARTS, 32, LANES), BF16),
            pltpu.VMEM((PARTS, PER, LANES), BF16),
            pltpu.VMEM((2, 1, LANES), jnp.int32),
            pltpu.VMEM((groups, LANES), F32),
            pltpu.VMEM((groups, LANES), F32),
            pltpu.VMEM((PARTS, PER, LANES), F32),
            pltpu.VMEM((4, LANES, LANES), BF16),
            pltpu.VMEM((4, LANES, LANES), F32),
            pltpu.VMEM((4, 8 * LANES, LANES), BF16),
            pltpu.VMEM((4, 8 * LANES, LANES), BF16),
            pltpu.VMEM((64, LANES), F32),
            pltpu.VMEM((64, LANES), F32),
            pltpu.VMEM((PARTS, PACK, LANES), F32),
            pltpu.VMEM((PARTS, PACK, LANES), F32),
            pltpu.VMEM((ROWS_Y, PACK, LANES), F32),
            pltpu.VMEM((ROWS_Z, PACK, LANES), F32),
            pltpu.VMEM((2, PACK, LANES), F32),
            dma((8,)), dma((8,)), dma((8,)), dma((8,)), dma((8,)), dma((8,)), dma((8,)),
            dma((8,)), dma((8,)), dma((2,)), dma((2,)),
            dma((8,)), dma((8,)), dma((8,)), dma((8,)), dma((12,)), dma((12,)),
        ],
        compiler_params=pltpu.CompilerParams(collective_id=0, has_side_effects=True),
        name="layer",
    )(vals, cot, filters, skip_gain.reshape(PER, LANES), seg_ids)
    streams = lax.axis_size("fsdp")
    length = rows * lax.axis_size("ctx")
    mirrored = jnp.concatenate([total_f[:, :1], total_f[:, :0:-1]], axis=1)
    total_f = jnp.where(lax.axis_index("fsdp") < HALF, mirrored, total_f)
    total_f = total_f / jnp.sqrt(F32(streams * length * 16))
    total_s = total_s / jnp.sqrt(F32(streams * length))
    return (mixed[None], grad[None], total_f, total_s.reshape(-1))


def solution(mesh):
    placed = (P("fsdp", "ctx", None), P("fsdp", "ctx", None), P("fsdp", "ctx"), P("fsdp", None), P("fsdp"))
    return jax.shard_map(
        shards,
        mesh=mesh,
        in_specs=placed,
        out_specs=(P("fsdp", "ctx", None), P("fsdp", "ctx", None), P("fsdp", None), P("fsdp")),
        check_vma=False,
    )
```

time: 775 us -> 78.8 us (0.10)
  blocking collectives: 470 us -> 0 us
  local copies, waits for them, and re-layouts: 205 us -> 5.52 us
  Pallas kernels: 0 us -> 71 us
  matrix products: 28.9 us -> 0 us
  other arithmetic: 28.6 us -> 1.26 us
  waiting for transfers between devices: 16.4 us -> 0 us
  between operations: 14.8 us -> 0.65 us
  starting transfers between devices: 8.27 us -> 0 us
    psum x1 -> x0, blocking collectives: 419 us -> none  [shards(): total_f, total_s = lax.psum((shard_f, shard_s), 'ctx')]
    reshape x36 -> x0, local copies, waits for them, and re-layouts: 115 us -> none  [the longest x16 45.7 us: diagonals(): bands = flat.reshape(count, rows, width + 1)[:, :, 1:taps + 1]]
    pallas_call x0 -> x1, Pallas kernels: none -> 71 us  [shards(): pl.pallas_call(kernel, out_shape=(jax.ShapeDtypeStruct((rows, channels),...]
    slice x21 -> x1, local copies, waits for them, and re-layouts: 34.1 us -> 0.79 us  [shards(): mirrored = jnp.concatenate([total_f[:, :1], total_f[:, :0:-1]], axis=1)]
    dot_general x24 -> x0, matrix products: 28.9 us -> none  [the longest x16 21.4 us: one_block(): jnp.einsum('tgc,sgc->gts', cot_part, val_part, preferred_element_type=jnp...]
    all_gather x2 -> x0, blocking collectives: 28 us -> none  [the longest x1 15.8 us: shards(): lax.all_gather(filters, 'fsdp', axis=0, tiled=True)]
    unnamed x1 -> x0, blocking collectives: 22.6 us -> none
    broadcast_in_dim x8 -> x0, local copies, waits for them, and re-layouts: 17.7 us -> none  [the longest x4 12.8 us: toeplitz(): jnp.broadcast_to(pattern[:, None, :], (count, rows, width + 1))]
  transfers between devices with their start and end apart: 4 -> 0, of which waited for: 1 -> 0; matrix products, arithmetic and copies ran while one was open for 1% -> 0% of each run, Pallas kernels for 0% -> 0%
where the time goes in v1:
time: 78.8 us; the launch traced here: 78.4 us
  Pallas kernels  71 us (90%)
  local copies, waits for them, and re-layouts  5.52 us (7%)
  other arithmetic  1.26 us (2%)
    pallas_call x1, Pallas kernels, shards(): pl.pallas_call(kernel, out_shape=(jax.ShapeDtypeStruct((rows, channels),...  71 us
    unnamed x8, local copies, waits for them, and re-layouts  4.65 us

profile of v1, /device:TPU:2, one launch (start us, length us, event | category | flops | bytes accessed | tf_op | source)
XLA Modules:
  0.0 78.4 jit_solution(7272729369646268028)
XLA Ops:
  0.6 71.0 %layer.1 = (bf16[128,4096]{1,0:T(8,128)(2,1)}, bf16[128,4096]{1,0:T(8,128)(2,1)}, f32[32,128]{1,0:T(8,128)}, f32[4,128]{1,0:T(4,128)}) custom-call(bf16[128,4096]{1,0:T(8,128)(2,1)} %bitcast.8, bf16[128,4096]{1,0:T(8,128)(2,1)} %bitcast.9, bf16[32,128]{1,0:T(8,128)(2,1)} %filt_ref.1, bf16[4,128]{1,0:T(4,128)(2,1)} %bitcast.13, s32[1,128]{1,0:T(1,128)} %ids_ref.1), custom_call_target="tpu_custom_call" | custom-call | tf_op jit(solution)/shard_map/layer/pallas_call | solution.py:264
  71.6 0.8 %slice.7 = f32[32,127]{1,0:T(8,128)S(1)} slice(f32[32,128]{1,0:T(8,128)} %get-tuple-element.10), slice={[0:32], [1:128]} | slice | bytes 32512 | tf_op jit(solution)/shard_map/slice | solution.py:302
  72.4 0.0 copy-start.1
  72.4 0.1 rev.3
  72.5 0.6 copy-done.1
  73.1 0.7 fusion
  73.8 0.0 copy-start.2
  73.8 0.7 copy-done.2
  74.5 0.6 multiply_bitcast_fusion
  75.1 0.0 copy-start
  75.1 2.4 %copy.11 = bf16[1,128,4096]{2,1,0:T(8,128)(2,1)} copy(bf16[1,128,4096]{2,1,0:T(8,128)(2,1)} %bitcast.11) | data formatting | bytes 2097152
  77.4 0.0 copy-done
  77.5 1.0 %copy.12 = bf16[1,128,4096]{2,1,0:T(8,128)(2,1)} copy(bf16[1,128,4096]{2,1,0:T(8,128)(2,1)S(1)} %bitcast.10) | data formatting | bytes 2097152
Async XLA Ops:
  72.4 0.7 copy-start.1
  73.8 0.7 copy-start.2
  75.1 2.4 %copy-start = (bf16[128,4096]{1,0:T(8,128)(2,1)S(1)}, bf16[128,4096]{1,0:T(8,128)(2,1)}, u32[]{:S(2)}) copy-start(bf16[128,4096]{1,0:T(8,128)(2,1)} %get-tuple-element.9) | copy-start | bytes 3145732

commit v2 on v1

--- a/solution.py
+++ b/solution.py
@@ -206,17 +206,14 @@
         skips[k] = skip_all[k].astype(F32)
         filt[32 * k : 32 * k + 32] = filt_all[k].astype(F32)
         flip[32 * k : 32 * k + 32] = jnp.dot(filt_all[k], turn, preferred_element_type=F32)
-    for chunk in range(CHUNKS):
-        if chunk < HALF:
-            c_copies[chunk].wait_recv()
-        else:
-            v_copies[chunk].wait_recv()
-
     build(0, filt, flip, bmask, lhs_a)
     last = CHUNKS * PER - 1
     stores = []
 
     def segment(first, stop):
+        for chunk in range(first, stop):
+            (c_copies if chunk < HALF else v_copies)[chunk].wait_recv()
+
         def two(j, carry):
             block = first * PER + 2 * j
             build(block + 1, filt, flip, bmask, lhs_b)

time: 78.8 us -> 70.8 us (0.90)
  the two profiles are of different devices: /device:TPU:2 before, /device:TPU:28 now
where the time goes in v2:
time: 70.8 us; the launch traced here: 70.5 us
  Pallas kernels  63 us (89%)
  local copies, waits for them, and re-layouts  5.52 us (8%)
  other arithmetic  1.26 us (2%)
    pallas_call x1, Pallas kernels, shards(): pl.pallas_call(kernel, out_shape=(jax.ShapeDtypeStruct((rows, channels),...  63 us
    unnamed x8, local copies, waits for them, and re-layouts  4.65 us

profile of v2, /device:TPU:28, one launch (start us, length us, event | category | flops | bytes accessed | tf_op | source)
XLA Modules:
  0.0 70.5 jit_solution(11383255447888746190)
XLA Ops:
  0.6 63.0 %layer.1 = (bf16[128,4096]{1,0:T(8,128)(2,1)}, bf16[128,4096]{1,0:T(8,128)(2,1)}, f32[32,128]{1,0:T(8,128)}, f32[4,128]{1,0:T(4,128)}) custom-call(bf16[128,4096]{1,0:T(8,128)(2,1)} %bitcast.8, bf16[128,4096]{1,0:T(8,128)(2,1)} %bitcast.9, bf16[32,128]{1,0:T(8,128)(2,1)} %filt_ref.1, bf16[4,128]{1,0:T(4,128)(2,1)} %bitcast.13, s32[1,128]{1,0:T(1,128)} %ids_ref.1), custom_call_target="tpu_custom_call" | custom-call | tf_op jit(solution)/shard_map/layer/pallas_call | solution.py:261
  63.7 0.8 %slice.7 = f32[32,127]{1,0:T(8,128)S(1)} slice(f32[32,128]{1,0:T(8,128)} %get-tuple-element.10), slice={[0:32], [1:128]} | slice | bytes 32512 | tf_op jit(solution)/shard_map/slice | solution.py:299
  64.5 0.0 copy-start.1
  64.5 0.1 rev.3
  64.5 0.6 copy-done.1
  65.2 0.7 fusion
  65.9 0.0 copy-start.2
  65.9 0.7 copy-done.2
  66.5 0.6 multiply_bitcast_fusion
  67.1 0.0 copy-start
  67.1 2.4 %copy.11 = bf16[1,128,4096]{2,1,0:T(8,128)(2,1)} copy(bf16[1,128,4096]{2,1,0:T(8,128)(2,1)} %bitcast.11) | data formatting | bytes 2097152
  69.5 0.0 copy-done
  69.5 1.0 %copy.12 = bf16[1,128,4096]{2,1,0:T(8,128)(2,1)} copy(bf16[1,128,4096]{2,1,0:T(8,128)(2,1)S(1)} %bitcast.10) | data formatting | bytes 2097152
Async XLA Ops:
  64.5 0.7 %copy-start.1 = (f32[32,128]{1,0:T(8,128)S(1)}, f32[32,128]{1,0:T(8,128)}, u32[]{:S(2)}) copy-start(f32[32,128]{1,0:T(8,128)} %get-tuple-element.10) | copy-start | bytes 49156
  65.9 0.7 copy-start.2
  67.1 2.4 %copy-start = (bf16[128,4096]{1,0:T(8,128)(2,1)S(1)}, bf16[128,4096]{1,0:T(8,128)(2,1)}, u32[]{:S(2)}) copy-start(bf16[128,4096]{1,0:T(8,128)(2,1)} %get-tuple-element.9) | copy-start | bytes 3145732
